TPU v7x, 32 devices: a whole 2x2x4 slice. The times are simulated.
32 devices in a mesh: gx: 8 (over y, x, core), gy: 4 (over z).
Axes of the slice: x: 2, y: 2, z: 4, core: 2. Of those that a mesh axis runs over, the one named last changes fastest.
Arguments:
- tokens: bfloat16 [3072, 2048], P('gx', 'gy'), may hold values from -40 to 40
- gain: float32 [2048], replicated, may hold values from 0.1 to 1.9
- w_qkv: bfloat16 [2048, 3, 16, 128], P('gx', None, 'gy'), may hold values from -0.176776695 to 0.176776695
- w_out: bfloat16 [2048, 2048], P('gx', 'gy'), may hold values from -0.125 to 0.125
- lengths: int32 [6], replicated, may hold values from 1 to 2048, 3072 in all
Outputs:
- mixed: bfloat16 [3072, 2048], P('gx', 'gy')
- key_cache: bfloat16 [3072, 16, 128], P('gx', 'gy')
- value_cache: bfloat16 [3072, 16, 128], P('gx', 'gy')
Inputs may be any that keep to these rules, and one draw needn't show every extreme that they name: lengths are positive and sum to 3072; the longest is exactly 2048.
All inputs are finite; a program needn't handle non-finite values.
Results may differ from a plain program's by a relative error of at most 0.012.
The roundings to bfloat16 on the way count: a program that leaves them out, or rounds other values in their place, can miss the bound.
Values may be sent and summed in bfloat16 or wider, within the bound.
No kernel may reach another device: no remote copies, remote signals or barrier semaphores. Data moves between devices by JAX's collectives and lax.ppermute only.
A program may use at most 64 MiB of HBM per device.

v0:
```python
import math
import jax
import jax.numpy as jnp
from jax import lax
from jax.sharding import PartitionSpec as P


def rotate(vectors, position):
    half = vectors.shape[-1] // 2
    freq = 10000.0 ** (-(2.0 * jnp.arange(half, dtype=jnp.float32)) / vectors.shape[-1])
    angle = position.astype(jnp.float32)[:, None, None] * freq[None, None, :]
    cosine = jnp.cos(angle)
    sine = jnp.sin(angle)
    first = vectors[..., :half]
    second = vectors[..., half:]
    return jnp.concatenate(
        [first * cosine - second * sine, second * cosine + first * sine], axis=-1
    )


def block_rows(count):
    size = count
    while size > 1024 and size % 2 == 0:
        size = size // 2
    return size


def local(tokens, gain, w_qkv, w_out, lengths):
    tok_dev = tokens.shape[0]
    hloc = w_qkv.shape[2]
    hsize = w_qkv.shape[3]
    whole = lax.all_gather(tokens, "gy", axis=1, tiled=True)
    wide = whole.astype(jnp.float32)
    meansq = jnp.mean(wide * wide, axis=-1, keepdims=True)
    normed = (wide * lax.rsqrt(meansq + 1e-06) * gain[None, :]).astype(jnp.bfloat16)
    piece = lax.all_gather(w_qkv, "gx", axis=0, tiled=True)
    columns = normed
    projected = jnp.dot(
        columns, piece.reshape(piece.shape[0], -1), preferred_element_type=jnp.float32
    )
    projected = projected.reshape(tok_dev, 3, hloc, hsize)
    mine = lax.axis_index("gx")
    glob = mine * tok_dev + jnp.arange(tok_dev, dtype=jnp.int32)
    doc_start = jnp.cumsum(lengths) - lengths
    begin = jnp.max(jnp.where(doc_start[None, :] <= glob[:, None], doc_start[None, :], 0), axis=1)
    position = glob - begin
    query = rotate(projected[:, 0], position).astype(jnp.bfloat16)
    keys_own = rotate(projected[:, 1], position).astype(jnp.bfloat16)
    vals_own = projected[:, 2].astype(jnp.bfloat16)
    scale = 1.0 / math.sqrt(hsize)

    def tile_step(state, keys_blk, vals_blk, first):
        running, totals, accum = state
        kidx = first + jnp.arange(keys_blk.shape[0], dtype=jnp.int32)
        score = (
            jnp.einsum("qhd,khd->hqk", query, keys_blk, preferred_element_type=jnp.float32) * scale
        )
        keep = (kidx[None, :] >= begin[:, None]) & (kidx[None, :] <= glob[:, None])
        score = jnp.where(keep[None], score, -1e30)
        newmax = jnp.maximum(running, jnp.max(score, axis=-1))
        weight = jnp.where(keep[None], jnp.exp(score - newmax[..., None]), 0.0)
        factor = jnp.exp(running - newmax)
        totals = totals * factor + jnp.sum(weight, axis=-1)
        update = jnp.einsum(
            "hqk,khd->hqd",
            weight.astype(jnp.bfloat16),
            vals_blk,
            preferred_element_type=jnp.float32,
        )
        accum = accum * factor[..., None] + update
        return (newmax, totals, accum)

    initial = (
        jnp.full((hloc, tok_dev), -1e30, jnp.float32),
        jnp.zeros((hloc, tok_dev), jnp.float32),
        jnp.zeros((hloc, tok_dev, hsize), jnp.float32),
    )
    keys_piece = lax.all_gather(keys_own, "gx", axis=0, tiled=True)
    vals_piece = lax.all_gather(vals_own, "gx", axis=0, tiled=True)
    count = keys_piece.shape[0]
    size = block_rows(count)

    def one_tile(number, inner):
        first = (number * size).astype(jnp.int32)
        keys_blk = lax.dynamic_slice_in_dim(keys_piece, first, size, 0)
        vals_blk = lax.dynamic_slice_in_dim(vals_piece, first, size, 0)
        return tile_step(inner, keys_blk, vals_blk, first)

    running, totals, accum = lax.fori_loop(0, count // size, one_tile, initial)
    attended = (accum / totals[..., None]).astype(jnp.bfloat16)
    attended = jnp.transpose(attended, (1, 0, 2)).reshape(tok_dev, hloc * hsize)
    all_heads = lax.all_gather(attended, "gy", axis=1, tiled=True)
    columns = all_heads
    mixed = jnp.dot(
        columns, lax.all_gather(w_out, "gx", axis=0, tiled=True), preferred_element_type=jnp.float32
    ).astype(jnp.bfloat16)
    return (mixed, keys_own, vals_own)


def solution(mesh):
    return jax.shard_map(
        local,
        mesh=mesh,
        in_specs=(P("gx", "gy"), P(), P("gx", None, "gy", None), P("gx", "gy"), P()),
        out_specs=(P("gx", "gy"), P("gx", "gy", None), P("gx", "gy", None)),
        check_vma=False,
    )
```

profile of v0, /device:TPU:0, one launch (start us, length us, event | category | flops | bytes accessed | tf_op | source)
XLA Modules:
  0.0 282.4 jit_solution(10697021689812042305)
XLA Ops:
  7.2 0.0 all-gather.8.cloned.1.call-start
  7.2 0.7 all-gather.8.cloned.1.call-update
  7.9 0.0 all-gather.10.cloned.1.call-start
  7.9 0.7 all-gather.10.cloned.1.call-update
  8.6 0.0 all-gather.12.cloned.1.call-start
  8.7 0.8 reduce-window.9
  9.5 0.7 bitcast_subtract_fusion
  10.2 0.1 select_reduce_fusion
  10.3 0.4 multiply_cosine_fusion
  10.7 38.7 %all-gather.8.cloned.1.call-done = bf16[384,2048]{1,0:T(8,128)(2,1)} async-done(((bf16[384,512]{1,0:T(8,128)(2,1)}), bf16[384,2048]{1,0:T(8,128)(2,1)}) %all-gather.8.cloned.1.call-update) | async-done | bytes 1572880 | tf_op jit(solution)/shard_map/all_gather | solution.py:32
  49.4 1.8 fusion.22
  51.2 0.0 copy-start.2
  51.2 44.5 %all-gather.10.cloned.1.call-done = bf16[2048,3,4,128]{3,2,1,0:T(4,128)(2,1)} async-done(((bf16[256,3,4,128]{3,2,1,0:T(4,128)(2,1)}), bf16[2048,3,4,128]{3,2,1,0:T(4,128)(2,1)}) %all-gather.10.cloned.1.call-update) | async-done | bytes 6291472 | tf_op jit(solution)/shard_map/all_gather | solution.py:36
  95.7 10.6 %copy.41 = bf16[2048,3,4,128]{0,3,2,1:T(8,128)(2,1)} copy(bf16[2048,3,4,128]{3,2,1,0:T(4,128)(2,1)} %all-gather.10.cloned.1.call-done) | data formatting | bytes 12582912 | tf_op jit(solution)/shard_map/reshape | solution.py:39
  106.3 0.0 copy-done.2
  106.3 6.2 %fusion.20 = f32[384,3,4,128]{0,3,2,1:T(8,128)S(1)} fusion(bf16[2048,3,4,128]{0,3,2,1:T(8,128)(2,1)} %copy.41, bf16[384,2048]{1,0:T(8,128)(2,1)} %all-gather.8.cloned.1.call-done, f32[2048]{0:T(1024)S(1)} %copy-done.2, f32[384]{0:T(512)S(1)} %add_rsqrt_fusion), kind=kOutput, calls=%fused_computation.25 | convolution fusion | flops 2419064832 | bytes 10233344 | tf_op jit(solution)/shard_map/dot_general | solution.py:38
  112.5 0.1 slice_bitcast_fusion
  112.6 0.2 subtract_convert_fusion
  112.8 0.8 pad_maximum_fusion
  113.6 0.0 all-gather.12.cloned.1.call-update
  113.6 0.0 all-gather.18.cloned.1.call-start
  113.7 0.8 slice.47
  114.5 0.0 all-gather.18.cloned.1.call-update
  114.5 0.0 all-gather.16.cloned.1.call-start
  114.6 0.5 all-gather.16.cloned.1.call-update
  115.1 0.0 all-gather.14.cloned.1.call-start
  115.2 0.2 copy.34
  115.5 31.2 %all-gather.12.cloned.1.call-done = bf16[3072,4,128]{0,2,1:T(8,128)(2,1)} async-done(((bf16[384,4,128]{0,2,1:T(8,128)(2,1)}), bf16[3072,4,128]{0,2,1:T(8,128)(2,1)}) %all-gather.12.cloned.1.call-update) | async-done | bytes 3145744 | tf_op jit(solution)/shard_map/all_gather | solution.py:78
  146.6 35.1 %all-gather.18.cloned.1.call-done = bf16[3072,1,4,128]{0,3,2,1:T(8,128)(2,1)} async-done(((bf16[384,1,4,128]{0,3,2,1:T(8,128)(2,1)}), bf16[3072,1,4,128]{0,3,2,1:T(8,128)(2,1)}) %all-gather.18.cloned.1.call-update) | async-done | bytes 3145744 | tf_op jit(solution)/shard_map/all_gather | solution.py:79
  181.8 50.4 %while.18 = (s32[]{:T(128)}, f32[4,384]{1,0:T(4,128)S(1)}, f32[4,384]{1,0:T(4,128)S(1)}, f32[4,384,128]{2,1,0:T(8,128)}, s32[384]{0:T(512)S(1)}, /*index=5*/bf16...) while((s32[]{:T(128)}, f32[4,384]{1,0:T(4,128)S(1)}, ...), condition=%wide.region_6.7_spmd.clone, body=%wide.region_3.6_spmd.clone.sunk | while | flops 620798592 | bytes 37858016 | solution.py:89
  181.8 0.3 compare_and_fusion.2
  182.1 4.4 %fusion.42 = (f32[4,384]{1,0:T(4,128)S(1)}, f32[4,768,384]{2,1,0:T(8,128)}) fusion(pred[384,768]{0,1:T(8,128)(4,1)S(1)} %compare_and_fusion.2, bf16[384,4,128]{2,0,1:T(8,128)(2,1)S(1)} %get-tuple-element.368, bf16[3072,4,128]{0,2,1:T(8,128)(2,1)} %get-tuple-element.367, s32[]{:T(128)S(6)} %select_n.63), kind=kOutput, calls=%fused_computation.3.clone.1 | convolution fusion | flops 305527296 | bytes 6199300 | tf_op jit(solution)/shard_map/while/body/eval_jaxpr/qhd,khd->hqk/dot_general | solution.py:56
  186.5 0.0 copy-start
  186.5 3.7 %fusion.43 = f32[4,384]{1,0:T(4,128)S(1)} fusion(f32[4,768,384]{2,1,0:T(8,128)} %get-tuple-element.333, f32[4,384]{1,0:T(4,128)S(1)} %select_maximum_fusion.2, pred[384,768]{0,1:T(8,128)(4,1)S(1)} %compare_and_fusion.2), kind=kLoop, calls=%fused_computation.5.clone.1 | loop fusion | flops 5896704 | bytes 5025792 | tf_op jit(solution)/shard_map/while/body/eval_jaxpr/reduce_sum | solution.py:63
  190.2 0.1 copy-done
  190.3 3.9 %fusion.45 = f32[4,384,128]{2,1,0:T(8,128)} fusion(f32[4,768,384]{2,1,0:T(8,128)S(1)} %copy-done, f32[4,384]{1,0:T(4,128)S(1)} %select_maximum_fusion.2, pred[384,768]{0,1:T(8,128)(4,1)S(1)} %compare_and_fusion.2, f32[4,384,128]{2,1,0:T(8,128)} %get-tuple-element.352, bf16[3072,4,128]{0,2,1:T(8,128)(2,1)} %get-tuple-element.369, s32[]{:T(128)S(6)} %select_n.63, ...), kind=kOutput, calls=%fused_computation.8.clone.1 | convolution fusion | flops 308477952 | bytes 7385093 | tf_op jit(solution)/shard_map/while/body/eval_jaxpr/hqk,khd->hqd/dot_general | solution.py:64
  194.2 0.3 compare_and_fusion.2
  194.5 4.4 %fusion.42 = (f32[4,384]{1,0:T(4,128)S(1)}, f32[4,768,384]{2,1,0:T(8,128)}) fusion(pred[384,768]{0,1:T(8,128)(4,1)S(1)} %compare_and_fusion.2, bf16[384,4,128]{2,0,1:T(8,128)(2,1)S(1)} %get-tuple-element.368, bf16[3072,4,128]{0,2,1:T(8,128)(2,1)} %get-tuple-element.367, s32[]{:T(128)S(6)} %select_n.63), kind=kOutput, calls=%fused_computation.3.clone.1 | convolution fusion | flops 305527296 | bytes 6199300 | tf_op jit(solution)/shard_map/while/body/eval_jaxpr/qhd,khd->hqk/dot_general | solution.py:56
  198.9 0.0 copy-start
  198.9 3.7 %fusion.43 = f32[4,384]{1,0:T(4,128)S(1)} fusion(f32[4,768,384]{2,1,0:T(8,128)} %get-tuple-element.333, f32[4,384]{1,0:T(4,128)S(1)} %select_maximum_fusion.2, pred[384,768]{0,1:T(8,128)(4,1)S(1)} %compare_and_fusion.2), kind=kLoop, calls=%fused_computation.5.clone.1 | loop fusion | flops 5896704 | bytes 5025792 | tf_op jit(solution)/shard_map/while/body/eval_jaxpr/reduce_sum | solution.py:63
  202.6 0.4 copy-done
  203.0 4.1 %fusion.45 = f32[4,384,128]{2,1,0:T(8,128)} fusion(f32[4,768,384]{2,1,0:T(8,128)S(1)} %copy-done, f32[4,384]{1,0:T(4,128)S(1)} %select_maximum_fusion.2, pred[384,768]{0,1:T(8,128)(4,1)S(1)} %compare_and_fusion.2, f32[4,384,128]{2,1,0:T(8,128)} %get-tuple-element.352, bf16[3072,4,128]{0,2,1:T(8,128)(2,1)} %get-tuple-element.369, s32[]{:T(128)S(6)} %select_n.63, ...), kind=kOutput, calls=%fused_computation.8.clone.1 | convolution fusion | flops 308477952 | bytes 7385093 | tf_op jit(solution)/shard_map/while/body/eval_jaxpr/hqk,khd->hqd/dot_general | solution.py:64
  207.1 0.3 compare_and_fusion.2
  207.4 4.4 %fusion.42 = (f32[4,384]{1,0:T(4,128)S(1)}, f32[4,768,384]{2,1,0:T(8,128)}) fusion(pred[384,768]{0,1:T(8,128)(4,1)S(1)} %compare_and_fusion.2, bf16[384,4,128]{2,0,1:T(8,128)(2,1)S(1)} %get-tuple-element.368, bf16[3072,4,128]{0,2,1:T(8,128)(2,1)} %get-tuple-element.367, s32[]{:T(128)S(6)} %select_n.63), kind=kOutput, calls=%fused_computation.3.clone.1 | convolution fusion | flops 305527296 | bytes 6199300 | tf_op jit(solution)/shard_map/while/body/eval_jaxpr/qhd,khd->hqk/dot_general | solution.py:56
  211.8 0.0 copy-start
  211.8 3.7 %fusion.43 = f32[4,384]{1,0:T(4,128)S(1)} fusion(f32[4,768,384]{2,1,0:T(8,128)} %get-tuple-element.333, f32[4,384]{1,0:T(4,128)S(1)} %select_maximum_fusion.2, pred[384,768]{0,1:T(8,128)(4,1)S(1)} %compare_and_fusion.2), kind=kLoop, calls=%fused_computation.5.clone.1 | loop fusion | flops 5896704 | bytes 5025792 | tf_op jit(solution)/shard_map/while/body/eval_jaxpr/reduce_sum | solution.py:63
  215.5 0.1 copy-done
  215.6 4.1 %fusion.45 = f32[4,384,128]{2,1,0:T(8,128)} fusion(f32[4,768,384]{2,1,0:T(8,128)S(1)} %copy-done, f32[4,384]{1,0:T(4,128)S(1)} %select_maximum_fusion.2, pred[384,768]{0,1:T(8,128)(4,1)S(1)} %compare_and_fusion.2, f32[4,384,128]{2,1,0:T(8,128)} %get-tuple-element.352, bf16[3072,4,128]{0,2,1:T(8,128)(2,1)} %get-tuple-element.369, s32[]{:T(128)S(6)} %select_n.63, ...), kind=kOutput, calls=%fused_computation.8.clone.1 | convolution fusion | flops 308477952 | bytes 7385093 | tf_op jit(solution)/shard_map/while/body/eval_jaxpr/hqk,khd->hqd/dot_general | solution.py:64
  219.7 0.3 compare_and_fusion.2
  220.0 4.4 %fusion.42 = (f32[4,384]{1,0:T(4,128)S(1)}, f32[4,768,384]{2,1,0:T(8,128)}) fusion(pred[384,768]{0,1:T(8,128)(4,1)S(1)} %compare_and_fusion.2, bf16[384,4,128]{2,0,1:T(8,128)(2,1)S(1)} %get-tuple-element.368, bf16[3072,4,128]{0,2,1:T(8,128)(2,1)} %get-tuple-element.367, s32[]{:T(128)S(6)} %select_n.63), kind=kOutput, calls=%fused_computation.3.clone.1 | convolution fusion | flops 305527296 | bytes 6199300 | tf_op jit(solution)/shard_map/while/body/eval_jaxpr/qhd,khd->hqk/dot_general | solution.py:56
  224.4 0.0 copy-start
  224.4 3.7 %fusion.43 = f32[4,384]{1,0:T(4,128)S(1)} fusion(f32[4,768,384]{2,1,0:T(8,128)} %get-tuple-element.333, f32[4,384]{1,0:T(4,128)S(1)} %select_maximum_fusion.2, pred[384,768]{0,1:T(8,128)(4,1)S(1)} %compare_and_fusion.2), kind=kLoop, calls=%fused_computation.5.clone.1 | loop fusion | flops 5896704 | bytes 5025792 | tf_op jit(solution)/shard_map/while/body/eval_jaxpr/reduce_sum | solution.py:63
  228.1 0.1 copy-done
  228.1 4.1 %fusion.45 = f32[4,384,128]{2,1,0:T(8,128)} fusion(f32[4,768,384]{2,1,0:T(8,128)S(1)} %copy-done, f32[4,384]{1,0:T(4,128)S(1)} %select_maximum_fusion.2, pred[384,768]{0,1:T(8,128)(4,1)S(1)} %compare_and_fusion.2, f32[4,384,128]{2,1,0:T(8,128)} %get-tuple-element.352, bf16[3072,4,128]{0,2,1:T(8,128)(2,1)} %get-tuple-element.369, s32[]{:T(128)S(6)} %select_n.63, ...), kind=kOutput, calls=%fused_computation.8.clone.1 | convolution fusion | flops 308477952 | bytes 7385093 | tf_op jit(solution)/shard_map/while/body/eval_jaxpr/hqk,khd->hqd/dot_general | solution.py:64
  232.2 0.0 copy-start.1
  232.2 1.4 copy.36
  233.7 0.8 divide_convert_fusion
  234.5 0.0 all-gather.14.cloned.1.call-update
  234.5 0.0 copy-done.1
  234.5 1.0 copy.37
  235.5 1.0 copy.38
  236.5 0.0 all-gather.16.cloned.1.call-done
  236.5 35.2 %all-gather.14.cloned.1.call-done = bf16[384,2048]{0,1:T(8,128)(2,1)} async-done(((bf16[384,512]{0,1:T(8,128)(2,1)}), bf16[384,2048]{0,1:T(8,128)(2,1)}) %all-gather.14.cloned.1.call-update) | async-done | bytes 1572880 | tf_op jit(solution)/shard_map/all_gather | solution.py:92
  271.7 3.8 %convolution_convert_fusion = bf16[384,512]{1,0:T(8,128)(2,1)} fusion(bf16[384,2048]{0,1:T(8,128)(2,1)} %all-gather.14.cloned.1.call-done, bf16[2048,512]{1,0:T(8,128)(2,1)} %all-gather.16.cloned.1.call-done), kind=kOutput, calls=%fused_computation.35 | convolution fusion | flops 805502976 | bytes 4063232 | tf_op jit(solution)/shard_map/dot_general | solution.py:94
  (29 shorter events, 0.3 us)
Async XLA Ops:
  7.2 42.2 %all-gather.8.cloned.1.call-start = ((), (), s32[]{:S(2)}) async-start(), calls=%async_computation | async-start | bytes 1966080 | tf_op jit(solution)/shard_map/all_gather | solution.py:32
  7.9 87.8 %all-gather.10.cloned.1.call-start = ((), (), s32[]{:S(2)}) async-start(), calls=%async_computation.1 | async-start | bytes 7077888 | tf_op jit(solution)/shard_map/all_gather | solution.py:36
  8.6 138.0 %all-gather.12.cloned.1.call-start = ((), (), s32[]{:S(2)}) async-start(), calls=%async_computation.2 | async-start | bytes 3538944 | tf_op jit(solution)/shard_map/all_gather | solution.py:78
  51.2 55.1 %copy-start.2 = (f32[2048]{0:T(1024)S(1)}, f32[2048]{0:T(1024)}, u32[]{:S(2)}) copy-start(f32[2048]{0:T(1024)} %param.8) | copy-start | bytes 24580
  113.6 68.1 %all-gather.18.cloned.1.call-start = ((), (), s32[]{:S(2)}) async-start(), calls=%async_computation.5 | async-start | bytes 3538944 | tf_op jit(solution)/shard_map/all_gather | solution.py:79
  114.5 122.0 %all-gather.16.cloned.1.call-start = ((), (), s32[]{:S(2)}) async-start(), calls=%async_computation.4 | async-start | bytes 2359296 | tf_op jit(solution)/shard_map/all_gather | solution.py:95
  115.1 156.6 %all-gather.14.cloned.1.call-start = ((), (), s32[]{:S(2)}) async-start(), calls=%async_computation.3 | async-start | bytes 1966080 | tf_op jit(solution)/shard_map/all_gather | solution.py:92
  186.5 3.8 %copy-start = (f32[4,768,384]{2,1,0:T(8,128)S(1)}, f32[4,768,384]{2,1,0:T(8,128)}, u32[]{:S(2)}) copy-start(f32[4,768,384]{2,1,0:T(8,128)} %get-tuple-element.333) | copy-start | bytes 14155780 | tf_op jit(solution)/shard_map/while
  198.9 4.1 %copy-start = (f32[4,768,384]{2,1,0:T(8,128)S(1)}, f32[4,768,384]{2,1,0:T(8,128)}, u32[]{:S(2)}) copy-start(f32[4,768,384]{2,1,0:T(8,128)} %get-tuple-element.333) | copy-start | bytes 14155780 | tf_op jit(solution)/shard_map/while
  211.8 3.8 %copy-start = (f32[4,768,384]{2,1,0:T(8,128)S(1)}, f32[4,768,384]{2,1,0:T(8,128)}, u32[]{:S(2)}) copy-start(f32[4,768,384]{2,1,0:T(8,128)} %get-tuple-element.333) | copy-start | bytes 14155780 | tf_op jit(solution)/shard_map/while
  224.4 3.8 %copy-start = (f32[4,768,384]{2,1,0:T(8,128)S(1)}, f32[4,768,384]{2,1,0:T(8,128)}, u32[]{:S(2)}) copy-start(f32[4,768,384]{2,1,0:T(8,128)} %get-tuple-element.333) | copy-start | bytes 14155780 | tf_op jit(solution)/shard_map/while
  232.2 2.3 copy-start.1
Sparse Core Ops, SparseCore 0:
  9.6 39.7 all-gather.7
  51.3 44.3 all-gather.9
  113.8 32.8 all-gather.11
  148.9 32.8 all-gather.17
  183.5 27.8 all-gather.15
  234.6 37.0 all-gather.13
where the time goes:
time: 283 us; the launch traced here: 282 us
  waiting for transfers between devices  187 us (66%)
  matrix products  43.8 us (15%)
  other arithmetic  21.6 us (8%)
  local copies, waits for them, and re-layouts  15.8 us (6%)
  between operations  14.2 us (5%)
    all_gather x1, waiting for transfers between devices, local(): piece = lax.all_gather(w_qkv, 'gx', axis=0, tiled=True)  44.5 us
    all_gather x1, waiting for transfers between devices, local(): whole = lax.all_gather(tokens, 'gy', axis=1, tiled=True)  38.7 us
    all_gather x1, waiting for transfers between devices, local(): all_heads = lax.all_gather(attended, 'gy', axis=1, tiled=True)  35.2 us
    all_gather x1, waiting for transfers between devices, local(): vals_piece = lax.all_gather(vals_own, 'gx', axis=0, tiled=True)  35.1 us
    all_gather x1, waiting for transfers between devices, local(): keys_piece = lax.all_gather(keys_own, 'gx', axis=0, tiled=True)  31.2 us
    dot_general x4, matrix products, tile_step(): jnp.einsum('qhd,khd->hqk', query, keys_blk, preferred_element_type=jnp.fl...  17.7 us
    dot_general x4, matrix products, tile_step(): jnp.einsum('hqk,khd->hqd', weight.astype(jnp.bfloat16), vals_blk, preferr...  16.1 us
    reduce_sum x4, other arithmetic, tile_step(): totals = totals * factor + jnp.sum(weight, axis=-1)  14.6 us
  transfers between devices with their start and end apart: 6, of which 5 were waited for; matrix products, arithmetic and copies ran while one was open for 21% of the time, Pallas kernels for 0%

commit v1 on v0

--- a/solution.py
+++ b/solution.py
@@ -3,6 +3,16 @@
 import jax.numpy as jnp
 from jax import lax
 from jax.sharding import PartitionSpec as P
+
+
+def gather_by_hops(x, name, d):
+    size = lax.axis_size(name)
+    current, blocks = (x, [x])
+    for _ in range(size - 1):
+        current = lax.ppermute(current, name, [(i, (i + 1) % size) for i in range(size)])
+        blocks.insert(0, current)
+    row_of_blocks = jnp.concatenate(blocks, axis=d)
+    return jnp.roll(row_of_blocks, (lax.axis_index(name) + 1) * x.shape[d], axis=d)
 
 
 def rotate(vectors, position):
@@ -29,7 +39,7 @@
     tok_dev = tokens.shape[0]
     hloc = w_qkv.shape[2]
     hsize = w_qkv.shape[3]
-    whole = lax.all_gather(tokens, "gy", axis=1, tiled=True)
+    whole = gather_by_hops(tokens, "gy", 1)
     wide = whole.astype(jnp.float32)
     meansq = jnp.mean(wide * wide, axis=-1, keepdims=True)
     normed = (wide * lax.rsqrt(meansq + 1e-06) * gain[None, :]).astype(jnp.bfloat16)

time: 283 us -> 246 us (0.87)
  waiting for transfers between devices: 187 us -> 145 us
  starting transfers between devices: 0.24 us -> 3.28 us
    all_gather x1 -> x0, waiting for transfers between devices: 38.7 us -> none  [local(): whole = lax.all_gather(tokens, 'gy', axis=1, tiled=True)]
    all_gather x1, waiting for transfers between devices: 44.5 us -> 10.1 us  [local(): piece = lax.all_gather(w_qkv, 'gx', axis=0, tiled=True)]
    ppermute x0 -> x3, waiting for transfers between devices: none -> 31.9 us  [gather_by_hops(): lax.ppermute(current, name, [(i, (i + 1) % size) for i in range(size)])]
    ppermute x0 -> x3, starting transfers between devices: none -> 3.08 us  [gather_by_hops(): lax.ppermute(current, name, [(i, (i + 1) % size) for i in range(size)])]
  transfers between devices with their start and end apart: 6 -> 8, of which waited for: 5 -> 7; matrix products, arithmetic and copies ran while one was open for 21% -> 24% of each run, Pallas kernels for 0% -> 0%
where the time goes in v1:
time: 246 us; the launch traced here: 245 us
  waiting for transfers between devices  145 us (59%)
  matrix products  43.7 us (18%)
  other arithmetic  20.9 us (8%)
  local copies, waits for them, and re-layouts  18.6 us (8%)
  between operations  14 us (6%)
  starting transfers between devices  3.28 us (1%)
    all_gather x1, waiting for transfers between devices, local(): vals_piece = lax.all_gather(vals_own, 'gx', axis=0, tiled=True)  35.3 us
    all_gather x1, waiting for transfers between devices, local(): all_heads = lax.all_gather(attended, 'gy', axis=1, tiled=True)  35.2 us
    ppermute x3, waiting for transfers between devices, gather_by_hops(): lax.ppermute(current, name, [(i, (i + 1) % size) for i in range(size)])  31.9 us
    all_gather x1, waiting for transfers between devices, local(): keys_piece = lax.all_gather(keys_own, 'gx', axis=0, tiled=True)  31.2 us
    dot_general x4, matrix products, tile_step(): jnp.einsum('qhd,khd->hqk', query, keys_blk, preferred_element_type=jnp.fl...  17.7 us
    dot_general x4, matrix products, tile_step(): jnp.einsum('hqk,khd->hqd', weight.astype(jnp.bfloat16), vals_blk, preferr...  16 us
    reduce_sum x4, other arithmetic, tile_step(): totals = totals * factor + jnp.sum(weight, axis=-1)  14.6 us
    reshape x1, local copies, waits for them, and re-layouts, local(): piece.reshape(piece.shape[0], -1)  10.6 us
  transfers between devices with their start and end apart: 8, of which 7 were waited for; matrix products, arithmetic and copies ran while one was open for 24% of the time, Pallas kernels for 0%

profile of v1, /device:TPU:0, one launch (start us, length us, event | category | flops | bytes accessed | tf_op | source)
XLA Modules:
  0.0 245.4 jit_solution(17997485241025590271)
XLA Ops:
  7.2 0.0 all-gather.7.cloned.1.call-start
  7.2 0.7 all-gather.7.cloned.1.call-update
  7.9 0.0 all-gather.9.cloned.1.call-start
  8.0 3.1 %collective-permute-start = (bf16[384,512]{1,0:T(8,128)(2,1)}, bf16[384,512]{1,0:T(8,128)(2,1)S(1)}, u32[]{:S(2)}, u32[]{:S(2)}) collective-permute-start(bf16[384,512]{1,0:T(8,128)(2,1)} %param.7), channel_id=1, source_target_pairs={{0,1},{1,2},{2,3},{3,0},{4,5},{5,6},{6,7},{7,4},{8,9},{9,10},{10,1... | collective-permute-start | bytes 1179656 | tf_op jit(solution)/shard_map/ppermute | solution.py:12
  11.0 11.3 %collective-permute-done = bf16[384,512]{1,0:T(8,128)(2,1)S(1)} collective-permute-done((bf16[384,512]{1,0:T(8,128)(2,1)}, bf16[384,512]{1,0:T(8,128)(2,1)S(1)}, u32[]{:S(2)}, u32[]{:S(2)}) %collective-permute-start) | collective-permute-done | bytes 393248 | tf_op jit(solution)/shard_map/ppermute | solution.py:12
  22.4 0.0 collective-permute-start.1
  22.4 0.8 reduce-window.9
  23.2 0.7 bitcast_subtract_fusion
  23.9 0.1 select_reduce_fusion
  24.0 10.5 %collective-permute-done.1 = bf16[384,512]{1,0:T(8,128)(2,1)S(1)} collective-permute-done((bf16[384,512]{1,0:T(8,128)(2,1)S(1)}, bf16[384,512]{1,0:T(8,128)(2,1)S(1)}, u32[]{:S(2)}, u32[]{:S(2)}) %collective-permute-start.1) | collective-permute-done | bytes 393248 | tf_op jit(solution)/shard_map/ppermute | solution.py:12
  34.5 0.0 collective-permute-start.2
  34.5 1.1 multiply_cosine_fusion
  35.6 10.1 %collective-permute-done.2 = bf16[384,512]{1,0:T(8,128)(2,1)S(1)} collective-permute-done((bf16[384,512]{1,0:T(8,128)(2,1)S(1)}, bf16[384,512]{1,0:T(8,128)(2,1)S(1)}, u32[]{:S(2)}, u32[]{:S(2)}) %collective-permute-start.2) | collective-permute-done | bytes 393248 | tf_op jit(solution)/shard_map/ppermute | solution.py:12
  45.8 0.0 copy-done.2
  46.1 1.6 copy-done.3
  47.7 0.4 fusion.22
  48.1 10.1 %all-gather.7.cloned.1.call-done = bf16[2048,3,4,128]{3,2,1,0:T(4,128)(2,1)} async-done(((bf16[256,3,4,128]{3,2,1,0:T(4,128)(2,1)}), bf16[2048,3,4,128]{3,2,1,0:T(4,128)(2,1)}) %all-gather.7.cloned.1.call-update) | async-done | bytes 6291472 | tf_op jit(solution)/shard_map/all_gather | solution.py:46
  58.1 10.6 %copy.41 = bf16[2048,3,4,128]{0,3,2,1:T(8,128)(2,1)} copy(bf16[2048,3,4,128]{3,2,1,0:T(4,128)(2,1)} %all-gather.7.cloned.1.call-done) | data formatting | bytes 12582912 | tf_op jit(solution)/shard_map/reshape | solution.py:49
  68.8 6.2 %fusion.20 = f32[384,3,4,128]{0,3,2,1:T(8,128)S(1)} fusion(bf16[2048,3,4,128]{0,3,2,1:T(8,128)(2,1)} %copy.41, f32[2048]{0:T(1024)S(1)} %copy-done.6, f32[384]{0:T(512)S(1)} %add_rsqrt_fusion, bf16[384,4096]{1,0:T(8,128)(2,1)} %copy-done.3, s32[]{:T(128)S(6)} %select_n.42), kind=kOutput, calls=%fused_computation.25 | convolution fusion | flops 2419064832 | bytes 10233348 | tf_op jit(solution)/shard_map/dot_general | solution.py:48
  75.0 0.0 copy-start.4
  75.0 0.0 copy-start.5
  75.0 0.1 slice_bitcast_fusion
  75.1 0.8 copy-done.4
  75.8 0.0 copy-done.5
  75.9 0.2 subtract_convert_fusion
  76.1 0.8 pad_maximum_fusion
  76.9 0.0 all-gather.9.cloned.1.call-update
  76.9 0.0 all-gather.15.cloned.1.call-start
  77.0 0.8 slice.47
  77.8 0.0 all-gather.15.cloned.1.call-update
  77.8 0.0 all-gather.13.cloned.1.call-start
  77.8 0.5 all-gather.13.cloned.1.call-update
  78.4 0.0 all-gather.11.cloned.1.call-start
  78.5 0.2 copy.34
  78.7 31.2 %all-gather.9.cloned.1.call-done = bf16[3072,4,128]{0,2,1:T(8,128)(2,1)} async-done(((bf16[384,4,128]{0,2,1:T(8,128)(2,1)}), bf16[3072,4,128]{0,2,1:T(8,128)(2,1)}) %all-gather.9.cloned.1.call-update) | async-done | bytes 3145744 | tf_op jit(solution)/shard_map/all_gather | solution.py:88
  109.9 35.3 %all-gather.15.cloned.1.call-done = bf16[3072,1,4,128]{0,3,2,1:T(8,128)(2,1)} async-done(((bf16[384,1,4,128]{0,3,2,1:T(8,128)(2,1)}), bf16[3072,1,4,128]{0,3,2,1:T(8,128)(2,1)}) %all-gather.15.cloned.1.call-update) | async-done | bytes 3145744 | tf_op jit(solution)/shard_map/all_gather | solution.py:89
  145.2 50.3 %while.18 = (s32[]{:T(128)}, f32[4,384]{1,0:T(4,128)S(1)}, f32[4,384]{1,0:T(4,128)S(1)}, f32[4,384,128]{2,1,0:T(8,128)}, s32[384]{0:T(512)S(1)}, /*index=5*/bf16...) while((s32[]{:T(128)}, f32[4,384]{1,0:T(4,128)S(1)}, ...), condition=%wide.region_6.7_spmd.clone, body=%wide.region_3.6_spmd.clone.sunk | while | flops 620798592 | bytes 37858016 | solution.py:99
  145.2 0.3 compare_and_fusion.2
  145.5 4.4 %fusion.44 = (f32[4,384]{1,0:T(4,128)S(1)}, f32[4,768,384]{2,1,0:T(8,128)}) fusion(pred[384,768]{0,1:T(8,128)(4,1)S(1)} %compare_and_fusion.2, bf16[384,4,128]{2,0,1:T(8,128)(2,1)S(1)} %get-tuple-element.368, bf16[3072,4,128]{0,2,1:T(8,128)(2,1)} %get-tuple-element.367, s32[]{:T(128)S(6)} %select_n.78), kind=kOutput, calls=%fused_computation.3.clone.1 | convolution fusion | flops 305527296 | bytes 6199300 | tf_op jit(solution)/shard_map/while/body/eval_jaxpr/qhd,khd->hqk/dot_general | solution.py:66
  149.9 3.7 %fusion.45 = f32[4,384]{1,0:T(4,128)S(1)} fusion(f32[4,768,384]{2,1,0:T(8,128)} %get-tuple-element.333, f32[4,384]{1,0:T(4,128)S(1)} %select_maximum_fusion.2, pred[384,768]{0,1:T(8,128)(4,1)S(1)} %compare_and_fusion.2), kind=kLoop, calls=%fused_computation.5.clone.1 | loop fusion | flops 5896704 | bytes 5025792 | tf_op jit(solution)/shard_map/while/body/eval_jaxpr/reduce_sum | solution.py:73
  153.6 0.1 copy-done
  153.7 3.8 %fusion.47 = f32[4,384,128]{2,1,0:T(8,128)} fusion(f32[4,768,384]{2,1,0:T(8,128)S(1)} %copy-done, f32[4,384]{1,0:T(4,128)S(1)} %select_maximum_fusion.2, pred[384,768]{0,1:T(8,128)(4,1)S(1)} %compare_and_fusion.2, f32[4,384,128]{2,1,0:T(8,128)} %get-tuple-element.352, bf16[3072,4,128]{0,2,1:T(8,128)(2,1)} %get-tuple-element.369, s32[]{:T(128)S(6)} %select_n.78, ...), kind=kOutput, calls=%fused_computation.8.clone.1 | convolution fusion | flops 308477952 | bytes 7385093 | tf_op jit(solution)/shard_map/while/body/eval_jaxpr/hqk,khd->hqd/dot_general | solution.py:74
  157.6 0.3 compare_and_fusion.2
  157.9 4.4 %fusion.44 = (f32[4,384]{1,0:T(4,128)S(1)}, f32[4,768,384]{2,1,0:T(8,128)}) fusion(pred[384,768]{0,1:T(8,128)(4,1)S(1)} %compare_and_fusion.2, bf16[384,4,128]{2,0,1:T(8,128)(2,1)S(1)} %get-tuple-element.368, bf16[3072,4,128]{0,2,1:T(8,128)(2,1)} %get-tuple-element.367, s32[]{:T(128)S(6)} %select_n.78), kind=kOutput, calls=%fused_computation.3.clone.1 | convolution fusion | flops 305527296 | bytes 6199300 | tf_op jit(solution)/shard_map/while/body/eval_jaxpr/qhd,khd->hqk/dot_general | solution.py:66
  162.3 3.7 %fusion.45 = f32[4,384]{1,0:T(4,128)S(1)} fusion(f32[4,768,384]{2,1,0:T(8,128)} %get-tuple-element.333, f32[4,384]{1,0:T(4,128)S(1)} %select_maximum_fusion.2, pred[384,768]{0,1:T(8,128)(4,1)S(1)} %compare_and_fusion.2), kind=kLoop, calls=%fused_computation.5.clone.1 | loop fusion | flops 5896704 | bytes 5025792 | tf_op jit(solution)/shard_map/while/body/eval_jaxpr/reduce_sum | solution.py:73
  166.0 0.4 copy-done
  166.4 4.1 %fusion.47 = f32[4,384,128]{2,1,0:T(8,128)} fusion(f32[4,768,384]{2,1,0:T(8,128)S(1)} %copy-done, f32[4,384]{1,0:T(4,128)S(1)} %select_maximum_fusion.2, pred[384,768]{0,1:T(8,128)(4,1)S(1)} %compare_and_fusion.2, f32[4,384,128]{2,1,0:T(8,128)} %get-tuple-element.352, bf16[3072,4,128]{0,2,1:T(8,128)(2,1)} %get-tuple-element.369, s32[]{:T(128)S(6)} %select_n.78, ...), kind=kOutput, calls=%fused_computation.8.clone.1 | convolution fusion | flops 308477952 | bytes 7385093 | tf_op jit(solution)/shard_map/while/body/eval_jaxpr/hqk,khd->hqd/dot_general | solution.py:74
  170.5 0.3 compare_and_fusion.2
  170.8 4.4 %fusion.44 = (f32[4,384]{1,0:T(4,128)S(1)}, f32[4,768,384]{2,1,0:T(8,128)}) fusion(pred[384,768]{0,1:T(8,128)(4,1)S(1)} %compare_and_fusion.2, bf16[384,4,128]{2,0,1:T(8,128)(2,1)S(1)} %get-tuple-element.368, bf16[3072,4,128]{0,2,1:T(8,128)(2,1)} %get-tuple-element.367, s32[]{:T(128)S(6)} %select_n.78), kind=kOutput, calls=%fused_computation.3.clone.1 | convolution fusion | flops 305527296 | bytes 6199300 | tf_op jit(solution)/shard_map/while/body/eval_jaxpr/qhd,khd->hqk/dot_general | solution.py:66
  175.2 3.7 %fusion.45 = f32[4,384]{1,0:T(4,128)S(1)} fusion(f32[4,768,384]{2,1,0:T(8,128)} %get-tuple-element.333, f32[4,384]{1,0:T(4,128)S(1)} %select_maximum_fusion.2, pred[384,768]{0,1:T(8,128)(4,1)S(1)} %compare_and_fusion.2), kind=kLoop, calls=%fused_computation.5.clone.1 | loop fusion | flops 5896704 | bytes 5025792 | tf_op jit(solution)/shard_map/while/body/eval_jaxpr/reduce_sum | solution.py:73
  178.9 0.1 copy-done
  178.9 4.1 %fusion.47 = f32[4,384,128]{2,1,0:T(8,128)} fusion(f32[4,768,384]{2,1,0:T(8,128)S(1)} %copy-done, f32[4,384]{1,0:T(4,128)S(1)} %select_maximum_fusion.2, pred[384,768]{0,1:T(8,128)(4,1)S(1)} %compare_and_fusion.2, f32[4,384,128]{2,1,0:T(8,128)} %get-tuple-element.352, bf16[3072,4,128]{0,2,1:T(8,128)(2,1)} %get-tuple-element.369, s32[]{:T(128)S(6)} %select_n.78, ...), kind=kOutput, calls=%fused_computation.8.clone.1 | convolution fusion | flops 308477952 | bytes 7385093 | tf_op jit(solution)/shard_map/while/body/eval_jaxpr/hqk,khd->hqd/dot_general | solution.py:74
  183.0 0.3 compare_and_fusion.2
  183.3 4.4 %fusion.44 = (f32[4,384]{1,0:T(4,128)S(1)}, f32[4,768,384]{2,1,0:T(8,128)}) fusion(pred[384,768]{0,1:T(8,128)(4,1)S(1)} %compare_and_fusion.2, bf16[384,4,128]{2,0,1:T(8,128)(2,1)S(1)} %get-tuple-element.368, bf16[3072,4,128]{0,2,1:T(8,128)(2,1)} %get-tuple-element.367, s32[]{:T(128)S(6)} %select_n.78), kind=kOutput, calls=%fused_computation.3.clone.1 | convolution fusion | flops 305527296 | bytes 6199300 | tf_op jit(solution)/shard_map/while/body/eval_jaxpr/qhd,khd->hqk/dot_general | solution.py:66
  187.7 3.7 %fusion.45 = f32[4,384]{1,0:T(4,128)S(1)} fusion(f32[4,768,384]{2,1,0:T(8,128)} %get-tuple-element.333, f32[4,384]{1,0:T(4,128)S(1)} %select_maximum_fusion.2, pred[384,768]{0,1:T(8,128)(4,1)S(1)} %compare_and_fusion.2), kind=kLoop, calls=%fused_computation.5.clone.1 | loop fusion | flops 5896704 | bytes 5025792 | tf_op jit(solution)/shard_map/while/body/eval_jaxpr/reduce_sum | solution.py:73
  191.4 0.1 copy-done
  191.5 4.1 %fusion.47 = f32[4,384,128]{2,1,0:T(8,128)} fusion(f32[4,768,384]{2,1,0:T(8,128)S(1)} %copy-done, f32[4,384]{1,0:T(4,128)S(1)} %select_maximum_fusion.2, pred[384,768]{0,1:T(8,128)(4,1)S(1)} %compare_and_fusion.2, f32[4,384,128]{2,1,0:T(8,128)} %get-tuple-element.352, bf16[3072,4,128]{0,2,1:T(8,128)(2,1)} %get-tuple-element.369, s32[]{:T(128)S(6)} %select_n.78, ...), kind=kOutput, calls=%fused_computation.8.clone.1 | convolution fusion | flops 308477952 | bytes 7385093 | tf_op jit(solution)/shard_map/while/body/eval_jaxpr/hqk,khd->hqd/dot_general | solution.py:74
  195.5 1.4 copy.36
  197.0 0.8 divide_convert_fusion
  197.8 0.0 all-gather.11.cloned.1.call-update
  197.8 1.0 copy.37
  198.9 1.0 copy.38
  199.8 35.2 %all-gather.11.cloned.1.call-done = bf16[384,2048]{0,1:T(8,128)(2,1)} async-done(((bf16[384,512]{0,1:T(8,128)(2,1)}), bf16[384,2048]{0,1:T(8,128)(2,1)}) %all-gather.11.cloned.1.call-update) | async-done | bytes 1572880 | tf_op jit(solution)/shard_map/all_gather | solution.py:102
  235.0 3.8 %convolution_convert_fusion = bf16[384,512]{1,0:T(8,128)(2,1)} fusion(bf16[384,2048]{0,1:T(8,128)(2,1)} %all-gather.11.cloned.1.call-done, bf16[2048,512]{1,0:T(8,128)(2,1)} %all-gather.13.cloned.1.call-done), kind=kOutput, calls=%fused_computation.36 | convolution fusion | flops 805502976 | bytes 4063232 | tf_op jit(solution)/shard_map/dot_general | solution.py:104
  (48 shorter events, 0.6 us)
Async XLA Ops:
  7.2 38.6 %copy-start.2 = (bf16[384,512]{1,0:T(8,128)(2,1)S(1)}, bf16[384,512]{1,0:T(8,128)(2,1)}, u32[]{:S(2)}) copy-start(bf16[384,512]{1,0:T(8,128)(2,1)} %param.7) | copy-start | bytes 1179652
  7.2 51.0 %all-gather.7.cloned.1.call-start = ((), (), s32[]{:S(2)}) async-start(), calls=%async_computation | async-start | bytes 7077888 | tf_op jit(solution)/shard_map/all_gather | solution.py:46
  7.9 102.0 %all-gather.9.cloned.1.call-start = ((), (), s32[]{:S(2)}) async-start(), calls=%async_computation.1 | async-start | bytes 3538944 | tf_op jit(solution)/shard_map/all_gather | solution.py:88
  8.0 14.4 %collective-permute-start = (bf16[384,512]{1,0:T(8,128)(2,1)}, bf16[384,512]{1,0:T(8,128)(2,1)S(1)}, u32[]{:S(2)}, u32[]{:S(2)}) collective-permute-start(bf16[384,512]{1,0:T(8,128)(2,1)} %param.7), channel_id=1, source_target_pairs={{0,1},{1,2},{2,3},{3,0},{4,5},{5,6},{6,7},{7,4},{8,9},{9,10},{10,1... | collective-permute-start | bytes 1179656 | tf_op jit(solution)/shard_map/ppermute | solution.py:12
  22.4 12.1 %collective-permute-start.1 = (bf16[384,512]{1,0:T(8,128)(2,1)S(1)}, bf16[384,512]{1,0:T(8,128)(2,1)S(1)}, u32[]{:S(2)}, u32[]{:S(2)}) collective-permute-start(bf16[384,512]{1,0:T(8,128)(2,1)S(1)} %collective-permute-done), channel_id=1, source_target_pairs={{0,1},{1,2},{2,3},{3,0},{4,5},{5,6},{6,7},{7,4},{8,9},{9,10},{10,1... | collective-permute-start | bytes 1179656 | tf_op jit(solution)/shard_map/ppermute | solution.py:12
  34.5 11.2 %collective-permute-start.2 = (bf16[384,512]{1,0:T(8,128)(2,1)S(1)}, bf16[384,512]{1,0:T(8,128)(2,1)S(1)}, u32[]{:S(2)}, u32[]{:S(2)}) collective-permute-start(bf16[384,512]{1,0:T(8,128)(2,1)S(1)} %collective-permute-done.1), channel_id=1, source_target_pairs={{0,1},{1,2},{2,3},{3,0},{4,5},{5,6},{6,7},{7,4},{8,9},{9,10},{10,1... | collective-permute-start | bytes 1179656 | tf_op jit(solution)/shard_map/ppermute | solution.py:12
  46.0 1.6 copy-start.3
  48.1 20.7 %copy-start.6 = (f32[2048]{0:T(1024)S(1)}, f32[2048]{0:T(1024)}, u32[]{:S(2)}) copy-start(f32[2048]{0:T(1024)} %param.8) | copy-start | bytes 24580
  75.0 0.9 copy-start.4
  75.0 0.9 copy-start.5
  76.9 68.3 %all-gather.15.cloned.1.call-start = ((), (), s32[]{:S(2)}) async-start(), calls=%async_computation.4 | async-start | bytes 3538944 | tf_op jit(solution)/shard_map/all_gather | solution.py:89
  77.8 122.0 %all-gather.13.cloned.1.call-start = ((), (), s32[]{:S(2)}) async-start(), calls=%async_computation.3 | async-start | bytes 2359296 | tf_op jit(solution)/shard_map/all_gather | solution.py:105
  78.4 156.7 %all-gather.11.cloned.1.call-start = ((), (), s32[]{:S(2)}) async-start(), calls=%async_computation.2 | async-start | bytes 1966080 | tf_op jit(solution)/shard_map/all_gather | solution.py:102
  149.9 3.8 %copy-start = (f32[4,768,384]{2,1,0:T(8,128)S(1)}, f32[4,768,384]{2,1,0:T(8,128)}, u32[]{:S(2)}) copy-start(f32[4,768,384]{2,1,0:T(8,128)} %get-tuple-element.333) | copy-start | bytes 14155780 | tf_op jit(solution)/shard_map/while
  162.3 4.1 %copy-start = (f32[4,768,384]{2,1,0:T(8,128)S(1)}, f32[4,768,384]{2,1,0:T(8,128)}, u32[]{:S(2)}) copy-start(f32[4,768,384]{2,1,0:T(8,128)} %get-tuple-element.333) | copy-start | bytes 14155780 | tf_op jit(solution)/shard_map/while
  175.2 3.8 %copy-start = (f32[4,768,384]{2,1,0:T(8,128)S(1)}, f32[4,768,384]{2,1,0:T(8,128)}, u32[]{:S(2)}) copy-start(f32[4,768,384]{2,1,0:T(8,128)} %get-tuple-element.333) | copy-start | bytes 14155780 | tf_op jit(solution)/shard_map/while
  187.7 3.8 %copy-start = (f32[4,768,384]{2,1,0:T(8,128)S(1)}, f32[4,768,384]{2,1,0:T(8,128)}, u32[]{:S(2)}) copy-start(f32[4,768,384]{2,1,0:T(8,128)} %get-tuple-element.333) | copy-start | bytes 14155780 | tf_op jit(solution)/shard_map/while
  195.5 2.3 copy-start.1
Sparse Core Ops, SparseCore 0:
  9.9 48.2 all-gather.6
  77.0 32.8 all-gather.8
  112.3 32.8 all-gather.14
  146.9 27.8 all-gather.12
  198.0 37.0 all-gather.10
